TPU v7x, 256 devices: a whole 4x4x8 slice. The times are simulated.
256 devices in a mesh: filt: 2 (over core), row: 4 (over x), col: 32 (over z, y).
Axes of the slice: x: 4, y: 4, z: 8, core: 2. Of those that a mesh axis runs over, the one named last changes fastest.
Arguments:
- particles: bfloat16 [24576, 256], P(('filt', 'row', 'col')), parts along dimension 0, may hold values from -6 to 6
- cotangent: bfloat16 [24576, 256], P(('filt', 'row', 'col')), parts along dimension 0, may hold values from -3 to 3
- row_potential: bfloat16 [24576], P(('filt', 'row', 'col')), parts along dimension 0, may hold values from -0.099609375 to 0.099609375
- col_potential: bfloat16 [24576], P(('filt', 'row', 'col')), parts along dimension 0, may hold values from -0.099609375 to 0.099609375
- weights: bfloat16 [24576], P(('filt', 'row', 'col')), parts along dimension 0, may hold values from 0.5 to 18
Outputs:
- grad_particles: bfloat16 [24576, 256], P(('filt', 'row', 'col')), parts along dimension 0
- grad_weights: float32 [24576], P(('filt', 'row', 'col')), parts along dimension 0
There are 2 independent parts, one for each index of `filt`. A program takes and returns all parts, laid end to end along the dimension named above; each array names one. Nothing has to cross between parts.
All inputs are finite; a program needn't handle non-finite values.
Results may differ from a plain program's by a relative error of at most 0.02.
Values may be sent and summed in bfloat16 or wider, within the bound.
No kernel may reach another device: no remote copies, remote signals or barrier semaphores. Data moves between devices by JAX's collectives and lax.ppermute only.
A program may use at most 64 MiB of HBM per device.

v0:
```python
import jax
import jax.numpy as jnp
from jax import lax
from jax.sharding import PartitionSpec as P

ITERS = 4
EPS = 0.09


def local(particles, cotangent, row_potential, col_potential, weights):
    row_parts, row_fpot, row_wts = (
        lax.all_gather(particles, "col", axis=0, tiled=True),
        lax.all_gather(row_potential, "col", axis=0, tiled=True),
        lax.all_gather(weights, "col", axis=0, tiled=True),
    )
    col_parts, col_grads, col_gpot = (
        lax.all_gather(particles, "row", axis=0, tiled=True),
        lax.all_gather(cotangent, "row", axis=0, tiled=True),
        lax.all_gather(col_potential, "row", axis=0, tiled=True),
    )
    own = particles.shape[0]
    width = particles.shape[1]
    rows = row_parts.shape[0]
    cols = col_parts.shape[0]
    blk = 512
    count = rows // blk
    row_float = row_parts.astype(jnp.float32)
    row_sq = jnp.sum(row_float * row_float, axis=1)
    col_float = col_parts.astype(jnp.float32)
    col_sq = jnp.sum(col_float * col_float, axis=1)
    fpot = row_fpot.astype(jnp.float32)
    gpot = col_gpot.astype(jnp.float32)
    stacked = jnp.concatenate([col_parts, col_grads], axis=0)
    items = (
        row_parts.reshape(count, blk, width),
        fpot.reshape(count, blk),
        row_sq.reshape(count, blk),
    )

    def plan_from(cross, pot_blk, sq_blk):
        cost = (sq_blk[:, None] + col_sq[None, :] - 2.0 * cross) / (2.0 * width)
        return jnp.exp((pot_blk[:, None] + gpot[None, :] - cost) / EPS)

    def plan_only(part_blk, pot_blk, sq_blk):
        cross = jnp.einsum("rd,cd->rc", part_blk, col_parts, preferred_element_type=jnp.float32)
        return plan_from(cross, pot_blk, sq_blk)

    def first(carry, item):
        part_blk, pot_blk, sq_blk = item
        both = jnp.einsum("rd,cd->rc", part_blk, stacked, preferred_element_type=jnp.float32)
        plan = plan_from(both[:, :cols], pot_blk, sq_blk)
        weighted = plan * both[:, cols:]
        return (
            (carry[0] + jnp.sum(plan, axis=0), carry[1] + jnp.sum(weighted, axis=0)),
            (jnp.sum(plan, axis=1), jnp.sum(weighted, axis=1)),
        )

    zeros_c = jnp.zeros((cols,), jnp.float32)
    (colmass_part, colph_part), (rowmass_part, rowph_part) = lax.scan(
        first, (zeros_c, zeros_c), items
    )
    rowmass, rowph = lax.psum((rowmass_part.reshape(rows), rowph_part.reshape(rows)), "col")
    colmass, colph = lax.psum((colmass_part, colph_part), "row")
    psi = zeros_c
    phi = jnp.zeros((rows,), jnp.float32)
    for step in range(ITERS):

        def apply_rows(carry, item):
            plan = plan_only(item[0], item[1], item[2])
            return (carry, jnp.dot(plan, psi, precision=lax.Precision.HIGHEST))

        unused, row_apply = lax.scan(apply_rows, jnp.zeros((), jnp.float32), items)
        row_total = lax.psum(row_apply.reshape(rows), "col")
        phi = -(rowph + row_total) / rowmass

        def apply_cols(acc, item):
            plan = plan_only(item[0], item[1], item[2])
            return (acc + jnp.dot(item[3], plan, precision=lax.Precision.HIGHEST), None)

        col_apply, unused_out = lax.scan(apply_cols, zeros_c, items + (phi.reshape(count, blk),))
        col_total = lax.psum(col_apply, "row")
        psi = -(colph + col_total) / colmass

    def last(acc, item):
        part_blk, pot_blk, sq_blk, phi_blk = item
        both = jnp.einsum("rd,cd->rc", part_blk, stacked, preferred_element_type=jnp.float32)
        plan = plan_from(both[:, :cols], pot_blk, sq_blk)
        mixed = plan * (both[:, cols:] + phi_blk[:, None] + psi[None, :])
        qrow = jnp.sum(mixed, axis=1)
        plan_bf = plan.astype(jnp.bfloat16)
        mixed_bf = mixed.astype(jnp.bfloat16)
        rowterm = jnp.dot(plan_bf, col_grads, preferred_element_type=jnp.float32)
        rowterm = rowterm + (
            jnp.dot(mixed_bf, col_parts, preferred_element_type=jnp.float32)
            - qrow[:, None] * part_blk.astype(jnp.float32)
        ) / (width * EPS)
        return (
            acc + jnp.einsum("rc,rd->cd", mixed_bf, part_blk, preferred_element_type=jnp.float32),
            rowterm,
        )

    col_acc, row_terms = lax.scan(
        last, jnp.zeros((cols, width), jnp.float32), items + (phi.reshape(count, blk),)
    )
    row_terms = row_terms.reshape(rows, width)
    start = lax.axis_index("col") * own
    summed = lax.psum(row_terms.astype(jnp.bfloat16), "col").astype(jnp.float32)
    row_own = lax.dynamic_slice_in_dim(summed, start, own, 0)
    col_own = lax.psum_scatter(
        col_acc.astype(jnp.bfloat16), "row", scatter_dimension=0, tiled=True
    ).astype(jnp.float32)
    grad_particles = (row_own + col_own / (width * EPS)).astype(jnp.bfloat16)
    phi_own = lax.dynamic_slice_in_dim(phi, start, own, 0)
    own_wts = weights.astype(jnp.float32)
    total, wphi = lax.psum((jnp.sum(own_wts), jnp.sum(own_wts * phi_own)), ("row", "col"))
    count_all = rows * lax.axis_size("row")
    grad_weights = -(count_all / total) * (phi_own - wphi / total)
    return (grad_particles, grad_weights)


def solution(mesh):
    return jax.shard_map(
        local,
        mesh=mesh,
        in_specs=(
            P(("filt", "row", "col"), None),
            P(("filt", "row", "col"), None),
            P(("filt", "row", "col")),
            P(("filt", "row", "col")),
            P(("filt", "row", "col")),
        ),
        out_specs=(P(("filt", "row", "col"), None), P(("filt", "row", "col"))),
        check_vma=False,
    )
```

profile of v0, /device:TPU:8, one launch (start us, length us, event | category | flops | bytes accessed | tf_op | source)
XLA Modules:
  0.0 1151.9 jit_solution(2241112115767740689)
XLA Ops:
  8.0 1.3 dynamic-slice
  10.7 75.0 %all-reduce = bf16[3072]{0:T(1024)(128)(2,1)S(1)} all-reduce(bf16[3072]{0:T(1024)(128)(2,1)S(1)} %dynamic-update-slice), channel_id=1, replica_groups=mesh['filt'=2,'row'=4,'col'=32] {'col'}, use_global_device_ids=true, to_apply=%add | all-reduce | flops 3072 | bytes 12288
  85.8 1.3 dynamic-slice.1
  88.5 10.5 all-reduce.1
  99.0 12.3 %all_gather.18 = bf16[384,256]{1,0:T(8,128)(2,1)S(1)} all-gather(bf16[96,256]{1,0:T(8,128)(2,1)} %param.25), channel_id=1, replica_groups=mesh['filt'=2,'row'=4,'col'=32] {'row'}, dimensions={0}, use_global_device_ids=true | all-gather | bytes 245760 | tf_op jit(solution)/shard_map/all_gather | solution.py:17
  111.3 12.3 %all_gather.19 = bf16[384,256]{1,0:T(8,128)(2,1)S(1)} all-gather(bf16[96,256]{1,0:T(8,128)(2,1)} %param.26), channel_id=1, replica_groups=mesh['filt'=2,'row'=4,'col'=32] {'row'}, dimensions={0}, use_global_device_ids=true | all-gather | bytes 245760 | tf_op jit(solution)/shard_map/all_gather | solution.py:18
  123.9 2.0 multiply_reduce_fusion
  125.9 7.0 while.118
  132.9 7.5 while.117
  140.5 139.2 %all-reduce.3 = (f32[3072]{0:T(1024)S(1)}, f32[3072]{0:T(1024)S(1)}, f32[3072]{0:T(1024)S(1)}) all-reduce(f32[3072]{0:T(1024)S(1)} %reshape.119, f32[3072]{0:T(1024)S(1)} %reshape.117, f32[3072]{0:T(1024)S(1)} %reshape.118), channel_id=1, replica_groups=mesh['filt'=2,'row'=4,'col'=32] {'col'}, use_global_device_ids=true, to_apply=%region_13.14 | all-reduce | flops 9216 | bytes 73728 | tf_op jit(solution)/shard_map/psum | solution.py:62
  279.7 5.8 while.119
  285.5 7.9 all-reduce.4
  294.0 7.5 while.124
  301.5 137.7 %psum.111 = f32[3072]{0:T(1024)S(1)} all-reduce(f32[3072]{0:T(1024)S(1)} %reshape.121), channel_id=1, replica_groups=mesh['filt'=2,'row'=4,'col'=32] {'col'}, use_global_device_ids=true, to_apply=%region_20.21 | all-reduce | flops 3072 | bytes 24576 | tf_op jit(solution)/shard_map/psum | solution.py:73
  439.2 5.8 while.120
  445.0 9.7 psum.112
  455.3 7.5 while.125
  462.8 137.7 %psum.113 = f32[3072]{0:T(1024)S(1)} all-reduce(f32[3072]{0:T(1024)S(1)} %reshape.123), channel_id=1, replica_groups=mesh['filt'=2,'row'=4,'col'=32] {'col'}, use_global_device_ids=true, to_apply=%region_26.27 | all-reduce | flops 3072 | bytes 24576 | tf_op jit(solution)/shard_map/psum | solution.py:73
  600.5 5.8 while.121
  606.3 7.7 psum.114
  614.7 7.5 while.126
  622.2 138.0 %psum.115 = f32[3072]{0:T(1024)S(1)} all-reduce(f32[3072]{0:T(1024)S(1)} %reshape.125), channel_id=1, replica_groups=mesh['filt'=2,'row'=4,'col'=32] {'col'}, use_global_device_ids=true, to_apply=%region_32.33 | all-reduce | flops 3072 | bytes 24576 | tf_op jit(solution)/shard_map/psum | solution.py:73
  760.2 5.8 while.122
  765.9 9.7 psum.116
  775.7 16.9 %while.123 = (s32[]{:T(128)}, f32[384,256]{1,0:T(8,128)S(1)}, bf16[6,512,256]{2,1,0:T(8,128)(2,1)}, f32[6,512]{1,0:T(8,128)S(1)}, f32[384]{0:T(512)S(1)}, /*inde...) while((s32[]{:T(128)}, f32[384,256]{1,0:T(8,128)S(1)}, ...), condition=%wide.region_38.39_spmd.clone, body=%wide.region_36.38_spmd.clone.sunk | while | flops 508100096 | bytes 9079975 | solution.py:102
  779.9 1.0 fusion.262
  782.7 1.0 fusion.262
  785.5 1.0 fusion.262
  788.4 1.0 fusion.262
  791.2 1.0 fusion.262
  794.8 346.5 %all-reduce.2 = (f32[]{:T(128)}, f32[]{:T(128)}) all-reduce(f32[]{:T(128)} %get-tuple-element.718, f32[]{:T(128)} %get-tuple-element.717), channel_id=1, replica_groups=mesh['filt'=2,'row'=4,'col'=32] {'row','col'}, use_global_device_ids=true, to_apply=%region_44.45 | all-reduce | flops 2 | bytes 16 | tf_op jit(solution)/shard_map/psum | solution.py:115
  1143.9 1.5 add_convert_fusion
  (338 shorter events, 76.8 us)
Async XLA Ops:
  7.2 116.7 %all-gather.2.cloned.1.call-start = ((), (), s32[]{:S(2)}) async-start(), calls=%async_computation.1 | async-start | bytes 1622016 | tf_op jit(solution)/shard_map/all_gather | solution.py:12
  7.9 1136.0 %reduce-scatter.2.cloned.1.call-start = ((), (), s32[]{:S(2)}) async-start(), calls=%async_computation.3 | async-start | bytes 245760 | tf_op jit(solution)/shard_map/reduce_scatter | solution.py:109
  123.8 2.1 copy-start
  293.4 0.6 copy-start.2
  454.7 0.6 copy-start.3
  614.1 0.6 copy-start.1
  792.6 1.5 copy-start.4
  793.4 350.6 %all-reduce.7.cloned.1.call-start = ((), (), s32[]{:S(2)}) async-start(), calls=%async_computation.2 | async-start | bytes 3145728 | tf_op jit(solution)/shard_map/psum | solution.py:107
Sparse Core Ops, SparseCore 0:
  10.6 78.8 all-gather.1
  793.5 18.2 reduce-scatter.1
  815.6 149.9 all-reduce.6
where the time goes:
time: 1150 us
  blocking collectives  1040 us (90%)
  matrix products  65.2 us (6%)
  between operations  17.3 us (2%)
  other arithmetic  12.4 us (1%)
    psum x3, blocking collectives, local(): row_total = lax.psum(row_apply.reshape(rows), 'col')  413 us
    psum x1, blocking collectives, local(): lax.psum((jnp.sum(own_wts), jnp.sum(own_wts * phi_own)), ('row', 'col'))  347 us
    psum x1, blocking collectives, local(): lax.psum((rowmass_part.reshape(rows), rowph_part.reshape(rows)), 'col')  139 us
    unnamed x2, blocking collectives  85.5 us
    psum x3, blocking collectives, local(): col_total = lax.psum(col_apply, 'row')  27.2 us
  transfers between devices with their start and end apart: 3, of which 0 were waited for; matrix products, arithmetic and copies ran while one was open for 0% of the time, Pallas kernels for 0%

commit v1 on v0

--- a/solution.py
+++ b/solution.py
@@ -112,7 +112,7 @@
     grad_particles = (row_own + col_own / (width * EPS)).astype(jnp.bfloat16)
     phi_own = lax.dynamic_slice_in_dim(phi, start, own, 0)
     own_wts = weights.astype(jnp.float32)
-    total, wphi = lax.psum((jnp.sum(own_wts), jnp.sum(own_wts * phi_own)), ("row", "col"))
+    total, wphi = lax.psum(lax.psum((jnp.sum(own_wts), jnp.sum(own_wts * phi_own)), "row"), "col")
     count_all = rows * lax.axis_size("row")
     grad_weights = -(count_all / total) * (phi_own - wphi / total)
     return (grad_particles, grad_weights)

time: 1150 us -> 977 us (0.85)
  blocking collectives: 1040 us -> 772 us
  waiting for transfers between devices: 1.4 us -> 96.5 us
    psum x1, blocking collectives: 347 us -> 73.8 us  [local(): lax.psum(lax.psum((jnp.sum(own_wts), jnp.sum(own_wts * phi_own)), 'row'),...]
    psum x1, waiting for transfers between devices: 0.01 us -> 95.2 us  [local(): summed = lax.psum(row_terms.astype(jnp.bfloat16), 'col').astype(jnp.float32)]
  transfers between devices with their start and end apart: 3 -> 3, of which waited for: 0 -> 1; matrix products, arithmetic and copies ran while one was open for 0% -> 1% of each run, Pallas kernels for 0% -> 0%
where the time goes in v1:
time: 977 us; the launch traced here: 975 us
  blocking collectives  772 us (79%)
  waiting for transfers between devices  96.5 us (10%)
  matrix products  65.3 us (7%)
  between operations  17.3 us (2%)
  other arithmetic  12.4 us (1%)
    psum x3, blocking collectives, local(): row_total = lax.psum(row_apply.reshape(rows), 'col')  413 us
    psum x1, blocking collectives, local(): lax.psum((rowmass_part.reshape(rows), rowph_part.reshape(rows)), 'col')  139 us
    psum x1, waiting for transfers between devices, local(): summed = lax.psum(row_terms.astype(jnp.bfloat16), 'col').astype(jnp.float32)  95.2 us
    unnamed x2, blocking collectives  85.5 us
    psum x1, blocking collectives, local(): lax.psum(lax.psum((jnp.sum(own_wts), jnp.sum(own_wts * phi_own)), 'row'),...  73.8 us
    psum x3, blocking collectives, local(): col_total = lax.psum(col_apply, 'row')  27.9 us
  transfers between devices with their start and end apart: 3, of which 1 were waited for; matrix products, arithmetic and copies ran while one was open for 1% of the time, Pallas kernels for 0%

profile of v1, /device:TPU:8, one launch (start us, length us, event | category | flops | bytes accessed | tf_op | source)
XLA Modules:
  0.0 975.1 jit_solution(8598477147861594348)
XLA Ops:
  8.0 1.3 dynamic-slice
  10.7 75.0 %all-reduce = bf16[3072]{0:T(1024)(128)(2,1)S(1)} all-reduce(bf16[3072]{0:T(1024)(128)(2,1)S(1)} %dynamic-update-slice), channel_id=1, replica_groups=mesh['filt'=2,'row'=4,'col'=32] {'col'}, use_global_device_ids=true, to_apply=%add | all-reduce | flops 3072 | bytes 12288
  85.8 1.3 dynamic-slice.1
  88.5 10.5 %all-reduce.1 = bf16[384]{0:T(512)(128)(2,1)S(1)} all-reduce(bf16[384]{0:T(512)(128)(2,1)S(1)} %dynamic-update-slice.1), channel_id=1, replica_groups=mesh['filt'=2,'row'=4,'col'=32] {'row'}, use_global_device_ids=true, to_apply=%add.1 | all-reduce | flops 384 | bytes 1536
  99.0 12.3 %all_gather.18 = bf16[384,256]{1,0:T(8,128)(2,1)S(1)} all-gather(bf16[96,256]{1,0:T(8,128)(2,1)} %param.25), channel_id=1, replica_groups=mesh['filt'=2,'row'=4,'col'=32] {'row'}, dimensions={0}, use_global_device_ids=true | all-gather | bytes 245760 | tf_op jit(solution)/shard_map/all_gather | solution.py:17
  111.3 12.3 %all_gather.19 = bf16[384,256]{1,0:T(8,128)(2,1)S(1)} all-gather(bf16[96,256]{1,0:T(8,128)(2,1)} %param.26), channel_id=1, replica_groups=mesh['filt'=2,'row'=4,'col'=32] {'row'}, dimensions={0}, use_global_device_ids=true | all-gather | bytes 245760 | tf_op jit(solution)/shard_map/all_gather | solution.py:18
  123.9 2.0 multiply_reduce_fusion
  125.9 7.0 while.118
  132.9 7.5 while.117
  140.5 139.2 %all-reduce.3 = (f32[3072]{0:T(1024)S(1)}, f32[3072]{0:T(1024)S(1)}, f32[3072]{0:T(1024)S(1)}) all-reduce(f32[3072]{0:T(1024)S(1)} %reshape.119, f32[3072]{0:T(1024)S(1)} %reshape.117, f32[3072]{0:T(1024)S(1)} %reshape.118), channel_id=1, replica_groups=mesh['filt'=2,'row'=4,'col'=32] {'col'}, use_global_device_ids=true, to_apply=%region_13.14 | all-reduce | flops 9216 | bytes 73728 | tf_op jit(solution)/shard_map/psum | solution.py:62
  279.7 5.8 while.119
  285.5 7.9 all-reduce.5
  294.0 7.5 while.124
  301.5 137.7 %psum.125 = f32[3072]{0:T(1024)S(1)} all-reduce(f32[3072]{0:T(1024)S(1)} %reshape.121), channel_id=1, replica_groups=mesh['filt'=2,'row'=4,'col'=32] {'col'}, use_global_device_ids=true, to_apply=%region_20.21 | all-reduce | flops 3072 | bytes 24576 | tf_op jit(solution)/shard_map/psum | solution.py:73
  439.2 5.8 while.120
  445.0 9.7 psum.126
  455.3 7.5 while.125
  462.8 137.7 %psum.127 = f32[3072]{0:T(1024)S(1)} all-reduce(f32[3072]{0:T(1024)S(1)} %reshape.123), channel_id=1, replica_groups=mesh['filt'=2,'row'=4,'col'=32] {'col'}, use_global_device_ids=true, to_apply=%region_26.27 | all-reduce | flops 3072 | bytes 24576 | tf_op jit(solution)/shard_map/psum | solution.py:73
  600.5 5.8 while.121
  606.4 7.7 psum.128
  614.7 7.5 while.126
  622.2 137.9 %psum.129 = f32[3072]{0:T(1024)S(1)} all-reduce(f32[3072]{0:T(1024)S(1)} %reshape.125), channel_id=1, replica_groups=mesh['filt'=2,'row'=4,'col'=32] {'col'}, use_global_device_ids=true, to_apply=%region_32.33 | all-reduce | flops 3072 | bytes 24576 | tf_op jit(solution)/shard_map/psum | solution.py:73
  760.2 5.8 while.122
  766.7 10.4 %all-reduce.4 = (f32[384]{0:T(512)S(1)}, f32[]{:T(128)}, f32[]{:T(128)}) all-reduce(f32[384]{0:T(512)S(1)} %get-tuple-element.512, f32[]{:T(128)} %get-tuple-element.718, f32[]{:T(128)} %get-tuple-element.717), channel_id=1, replica_groups=mesh['filt'=2,'row'=4,'col'=32] {'row'}, use_global_device_ids=true, to_apply=%region_35.36 | all-reduce | flops 386 | bytes 3088 | tf_op jit(solution)/shard_map/psum | solution.py:81
  777.1 16.9 %while.123 = (s32[]{:T(128)}, f32[384,256]{1,0:T(8,128)S(1)}, bf16[6,512,256]{2,1,0:T(8,128)(2,1)}, f32[6,512]{1,0:T(8,128)S(1)}, f32[384]{0:T(512)S(1)}, /*inde...) while((s32[]{:T(128)}, f32[384,256]{1,0:T(8,128)S(1)}, ...), condition=%wide.region_38.39_spmd.clone, body=%wide.region_36.38_spmd.clone.sunk | while | flops 508100096 | bytes 9079975 | solution.py:102
  784.2 1.0 fusion.262
  787.0 1.0 fusion.262
  789.8 1.0 fusion.262
  792.6 1.0 fusion.262
  795.5 73.8 %all-reduce.2 = (f32[]{:T(128)}, f32[]{:T(128)}) all-reduce(f32[]{:T(128)} %get-tuple-element.915, f32[]{:T(128)} %get-tuple-element.916), channel_id=1, replica_groups=mesh['filt'=2,'row'=4,'col'=32] {'col'}, use_global_device_ids=true, to_apply=%region_46.47 | all-reduce | flops 2 | bytes 16 | tf_op jit(solution)/shard_map/psum | solution.py:115
  871.9 95.2 %all-reduce.8.cloned.1.call-done = bf16[3072,256]{1,0:T(8,128)(2,1)} async-done(((bf16[3072,256]{1,0:T(8,128)(2,1)}), bf16[3072,256]{1,0:T(8,128)(2,1)}) %all-reduce.8.cloned.1.call-update) | async-done | bytes 1572880 | tf_op jit(solution)/shard_map/psum | solution.py:107
  967.1 1.5 add_convert_fusion
  (338 shorter events, 77.9 us)
Async XLA Ops:
  7.2 116.7 %all-gather.2.cloned.1.call-start = ((), (), s32[]{:S(2)}) async-start(), calls=%async_computation.1 | async-start | bytes 1622016 | tf_op jit(solution)/shard_map/all_gather | solution.py:12
  7.9 864.0 %reduce-scatter.2.cloned.1.call-start = ((), (), s32[]{:S(2)}) async-start(), calls=%async_computation.3 | async-start | bytes 245760 | tf_op jit(solution)/shard_map/reduce_scatter | solution.py:109
  123.9 2.1 copy-start
  293.4 0.6 copy-start.2
  454.7 0.6 copy-start.3
  614.1 0.6 copy-start.1
  760.2 5.8 copy-start.4
  794.8 172.3 %all-reduce.8.cloned.1.call-start = ((), (), s32[]{:S(2)}) async-start(), calls=%async_computation.2 | async-start | bytes 3145728 | tf_op jit(solution)/shard_map/psum | solution.py:107
Sparse Core Ops, SparseCore 0:
  10.6 78.8 all-gather.1
  794.9 18.1 reduce-scatter.1
  817.0 150.0 all-reduce.7
